TPU v7x, 32 devices: a whole 2x2x4 slice. The times are simulated.
32 devices in a mesh: ctx: 8 (over y, x, core), tp: 4 (over z).
Axes of the slice: x: 2, y: 2, z: 4, core: 2. Of those that a mesh axis runs over, the one named last changes fastest.
Arguments:
- query_mr: bfloat16 [2048, 8192], P('ctx', 'tp'), may hold values from -6 to 6
- key_mr: bfloat16 [2048, 8192], P('ctx', 'tp'), may hold values from -6 to 6
- value_mr: bfloat16 [2048, 8192], P('ctx', 'tp'), may hold values from -6 to 6
- query_li: bfloat16 [2048, 8192], P('ctx', 'tp'), may hold values from -6 to 6
- key_li: bfloat16 [2048, 8192], P('ctx', 'tp'), may hold values from -6 to 6
- cotangent: bfloat16 [2048, 8192], P('ctx', 'tp'), may hold values from -6 to 6
- mr_taps: float32 [128, 8192], P(None, 'tp'), may hold values from -0.5 to 0.5
- decay_rates: float32 [8], replicated, may hold values from 4.8828126e-05 to 0.03
- residues: float32 [8, 8192], P(None, 'tp'), may hold values from -2 to 2
Outputs:
- grad_query_mr: bfloat16 [2048, 8192], P('ctx', 'tp')
- grad_key_mr: bfloat16 [2048, 8192], P('ctx', 'tp')
- grad_value_mr: bfloat16 [2048, 8192], P('ctx', 'tp')
- grad_query_li: bfloat16 [2048, 8192], P('ctx', 'tp')
- grad_key_li: bfloat16 [2048, 8192], P('ctx', 'tp')
- grad_taps: float32 [128, 8192], P(None, 'tp')
- grad_residues: float32 [8, 8192], P(None, 'tp')
All inputs are finite; a program needn't handle non-finite values.
Results may differ from a plain program's by a relative error of at most 0.001.
Values may be sent and summed in bfloat16 or wider, within the bound.
A program may use at most 128 MiB of HBM per device.

v0:
```python
import math
import jax
import jax.numpy as jnp
from jax import lax
from jax.sharding import PartitionSpec as P

BLOCK = 128
highest = lax.Precision.HIGHEST


def from_behind(value, axis, by):
    size = lax.axis_size(axis)
    pairs = [(i, i + by) for i in range(size) if 0 <= i + by < size]
    return lax.ppermute(value, axis, pairs)


def depthwise(signal, kernel):
    channels = signal.shape[1]
    output = lax.conv_general_dilated(
        signal[None],
        kernel[:, None, :],
        (1,),
        "VALID",
        dimension_numbers=("NWC", "WIO", "NWC"),
        feature_group_count=channels,
        precision=highest,
    )
    return output[0]


def linked(earlier, later):
    return (earlier[0] * later[1] + later[0], earlier[1] * later[1])


def modal_terms(inputs, cotangents, decay_rates, residues, block_len):
    length, channels = inputs.shape
    blocks = length // block_len
    in_blocks = inputs.reshape(blocks, block_len, channels)
    co_blocks = cotangents.reshape(blocks, block_len, channels)
    places = jnp.arange(block_len, dtype=jnp.float32)
    offsets = places[:, None] - places[None, :]
    modes = decay_rates.shape[0]

    def one_mode(mode, state):
        conv_sum, back_sum, residue_grad, end_rows, start_rows = state
        decay_rate = decay_rates[mode]
        residue_row = lax.dynamic_index_in_dim(residues, mode, 0, keepdims=False)
        mode_scale = jnp.sqrt(-jnp.expm1(-2.0 * decay_rate))
        toeplitz = jnp.where(
            offsets >= 0.0, mode_scale * jnp.exp(-decay_rate * jnp.maximum(offsets, 0.0)), 0.0
        )
        block_pows = jnp.full((blocks, 1), jnp.exp(-decay_rate * block_len), jnp.float32)
        forward = jnp.einsum("tj,bjc->btc", toeplitz, in_blocks, precision=highest)
        backward = jnp.einsum("jt,bjc->btc", toeplitz, co_blocks, precision=highest)
        forward_incl = lax.associative_scan(linked, (forward[:, -1], block_pows))[0]
        backward_incl = lax.associative_scan(linked, (backward[:, 0], block_pows), reverse=True)[0]
        zero_row = jnp.zeros((1, channels), jnp.float32)
        forward_in = jnp.concatenate([zero_row, forward_incl[:-1]], 0)
        backward_in = jnp.concatenate([backward_incl[1:], zero_row], 0)
        lead_pows = jnp.exp(-decay_rate * (places + 1.0))
        tail_pows = jnp.exp(-decay_rate * (block_len - places))
        states = (forward + lead_pows[None, :, None] * forward_in[:, None, :]).reshape(
            length, channels
        )
        reverse_states = (backward + tail_pows[None, :, None] * backward_in[:, None, :]).reshape(
            length, channels
        )
        conv_sum = conv_sum + residue_row[None, :] * states
        back_sum = back_sum + residue_row[None, :] * reverse_states
        residue_grad = lax.dynamic_update_index_in_dim(
            residue_grad, jnp.sum(inputs * reverse_states, 0), mode, 0
        )
        end_rows = lax.dynamic_update_index_in_dim(end_rows, states[length - 1], mode, 0)
        start_rows = lax.dynamic_update_index_in_dim(start_rows, reverse_states[0], mode, 0)
        return (conv_sum, back_sum, residue_grad, end_rows, start_rows)

    zero_field = jnp.zeros((length, channels), jnp.float32)
    zero_modes = jnp.zeros((modes, channels), jnp.float32)
    return lax.fori_loop(
        0, modes, one_mode, (zero_field, zero_field, zero_modes, zero_modes, zero_modes)
    )


def per_device(
    query_mr, key_mr, value_mr, query_li, key_li, cotangent, mr_taps, decay_rates, residues
):
    length, channels = query_mr.shape
    taps_len = mr_taps.shape[0]
    rim_rows = taps_len - 1
    devices_ctx = lax.axis_size("ctx")
    seq_len = length * devices_ctx
    prior_key, prior_value = from_behind(
        (key_mr[length - rim_rows :], value_mr[length - rim_rows :]), "ctx", 1
    )
    key_first = key_mr.astype(jnp.float32)
    value_first = value_mr.astype(jnp.float32)
    query_first = query_mr.astype(jnp.float32)
    mixed_in = jnp.concatenate([prior_key, key_mr], 0).astype(jnp.float32) * jnp.concatenate(
        [prior_value, value_mr], 0
    ).astype(jnp.float32)
    mr_conv = depthwise(mixed_in, mr_taps[::-1])
    mr_out = query_first * mr_conv
    key_second = key_li.astype(jnp.float32)
    cotan = cotangent.astype(jnp.float32)
    li_input = key_second * mr_out
    li_cotan = cotan * query_li.astype(jnp.float32)
    regrouped = lax.all_to_all(
        jnp.stack([li_input, li_cotan]), "ctx", split_axis=2, concat_axis=1, tiled=True
    )
    piece_cols = channels // devices_ctx
    local_residues = lax.dynamic_slice_in_dim(
        residues, lax.axis_index("ctx") * piece_cols, piece_cols, 1
    )
    conv_seq, back_seq, residue_piece, unused_ends, unused_starts = modal_terms(
        regrouped[0], regrouped[1], decay_rates, local_residues, BLOCK
    )
    returned = lax.all_to_all(
        jnp.stack([conv_seq, back_seq]), "ctx", split_axis=1, concat_axis=2, tiled=True
    )
    li_conv = returned[0]
    li_back = returned[1]
    residue_sum = lax.all_gather(residue_piece, "ctx", axis=1, tiled=True)
    grad_query_li = (cotan * li_conv).astype(jnp.bfloat16)
    grad_key_li = (mr_out * li_back).astype(jnp.bfloat16)
    mr_grad = cotan + key_second * li_back
    grad_query_mr = (mr_grad * mr_conv).astype(jnp.bfloat16)
    mr_cotan = mr_grad * query_first
    next_rows = from_behind(mr_cotan[:rim_rows], "ctx", -1)
    mixed_grad = depthwise(jnp.concatenate([mr_cotan, next_rows], 0), mr_taps)
    grad_key_mr = (mixed_grad * value_first).astype(jnp.bfloat16)
    grad_value_mr = (mixed_grad * key_first).astype(jnp.bfloat16)
    tap_part = depthwise(mixed_in, mr_cotan)[::-1]
    tap_sum = lax.psum(tap_part, "ctx")
    factor = 1.0 / math.sqrt(seq_len)
    return (
        grad_query_mr,
        grad_key_mr,
        grad_value_mr,
        grad_query_li,
        grad_key_li,
        tap_sum * factor,
        residue_sum * factor,
    )


def solution(mesh):
    placed = (
        P("ctx", "tp"),
        P("ctx", "tp"),
        P("ctx", "tp"),
        P("ctx", "tp"),
        P("ctx", "tp"),
        P("ctx", "tp"),
        P(None, "tp"),
        P(),
        P(None, "tp"),
    )
    return jax.shard_map(
        per_device,
        mesh=mesh,
        in_specs=placed,
        out_specs=(
            P("ctx", "tp"),
            P("ctx", "tp"),
            P("ctx", "tp"),
            P("ctx", "tp"),
            P("ctx", "tp"),
            P(None, "tp"),
            P(None, "tp"),
        ),
        check_vma=False,
    )
```

profile of v0, /device:TPU:0, one launch (start us, length us, event | category | flops | bytes accessed | tf_op | source)
XLA Modules:
  0.0 570.9 jit_solution(17721856543120809470)
XLA Ops:
  13.7 5.3 collective-permute-start.1
  19.0 8.9 %rev.15 = f32[128,2048]{1,0:T(8,128)} reverse(f32[128,2048]{1,0:T(8,128)} %param.17), dimensions={0} | reverse | bytes 2097152 | tf_op jit(solution)/shard_map/rev | solution.py:101
  31.3 21.5 %fusion.49 = f32[1,256,2048]{2,0,1:T(1,128)S(1)} fusion(f32[1,383,2048]{2,1,0:T(8,128)S(1)} %convert_multiply_fusion, f32[128,1,2048]{2,0,1:T(8,128)S(1)} %bitcast.140), kind=kOutput, calls=%fused_computation.100 | convolution fusion | flops 805306368 | bytes 6283264 | tf_op jit(solution)/shard_map/conv_general_dilated | solution.py:19
  56.9 7.3 %copy.48 = f32[2,256,2048]{1,0,2:T(2,128)} copy(f32[2,256,2048]{2,1,0:T(8,128)} %pad_maximum_fusion.6) | data formatting | bytes 8388608 | tf_op jit(solution)/shard_map/stack | solution.py:108
  64.1 4.6 all-to-all-start
  68.8 49.0 %all-to-all-done = f32[2,256,2048]{1,0,2:T(2,128)} async-done(((f32[2,256,2048]{1,0,2:T(2,128)}), f32[2,256,2048]{1,0,2:T(2,128)}, u32[]{:S(2)}, u32[]{:S(2)}) %all-to-all-start) | async-done | bytes 4194336 | tf_op jit(solution)/shard_map/all_to_all | solution.py:107
  117.8 9.6 %fusion.58 = (f32[1,8,256,256]{2,0,3,1:T(1,128)}, f32[1,8,256,256]{2,0,3,1:T(1,128)}) fusion(f32[2,8,256,256]{2,0,3,1:T(2,128)} %bitcast.8), kind=kLoop, calls=%fused_computation.113 | loop fusion | bytes 8388608 | tf_op jit(solution)/shard_map/slice | solution.py:115
  127.4 4.5 copy.49
  131.9 6.0 %copy.50 = f32[1,8,256,256]{3,2,1,0:T(8,128)} copy(f32[1,8,256,256]{2,0,3,1:T(1,128)} %get-tuple-element.304) | data formatting | bytes 4194304 | tf_op jit(solution)/shard_map/slice | solution.py:115
  138.0 240.8 %while.19 = (s32[]{:T(128)}, f32[2048,256]{1,0:T(8,128)}, f32[2048,256]{1,0:T(8,128)}, f32[8,256]{1,0:T(8,128)S(1)}, f32[8,256]{1,0:T(8,128)S(1)}, /*index=5*/f3...) while((s32[]{:T(128)}, f32[2048,256]{1,0:T(8,128)}, ...), condition=%wide.region_2.3_spmd.clone.clone, body=%wide.region_0.2_spmd.clone.clone.sunk | while | flops 1617155328 | bytes 74435056 | solution.py:79
  155.4 4.0 fusion.89
  162.0 4.9 fusion.90
  184.4 4.0 fusion.89
  191.0 6.2 %fusion.90 = (f32[2048,256]{1,0:T(8,128)}, f32[2048,256]{1,0:T(8,128)}) fusion(f32[16,128,256]{2,1,0:T(8,128)} %copy.106, f32[2048,256]{1,0:T(8,128)} %get-tuple-element.414, f32[256]{0:T(256)S(1)} %bitcast.142, pred[]{:T(512)S(6)} %compare.24, f32[16,128,256]{2,1,0:T(8,128)} %multiply_add_fusion.22, f32[2048,256]{1,0:T(8,128)} %get-tuple-element.413), kind=kLoop, calls=%fused_computation.3.clone.1 | loop fusion | flops 3145728 | bytes 12583937 | tf_op jit(solution)/shard_map/while/body/eval_jaxpr/add | solution.py:69
  214.6 4.0 fusion.89
  221.3 6.2 %fusion.90 = (f32[2048,256]{1,0:T(8,128)}, f32[2048,256]{1,0:T(8,128)}) fusion(f32[16,128,256]{2,1,0:T(8,128)} %copy.106, f32[2048,256]{1,0:T(8,128)} %get-tuple-element.414, f32[256]{0:T(256)S(1)} %bitcast.142, pred[]{:T(512)S(6)} %compare.24, f32[16,128,256]{2,1,0:T(8,128)} %multiply_add_fusion.22, f32[2048,256]{1,0:T(8,128)} %get-tuple-element.413), kind=kLoop, calls=%fused_computation.3.clone.1 | loop fusion | flops 3145728 | bytes 12583937 | tf_op jit(solution)/shard_map/while/body/eval_jaxpr/add | solution.py:69
  244.9 4.0 fusion.89
  251.5 6.2 %fusion.90 = (f32[2048,256]{1,0:T(8,128)}, f32[2048,256]{1,0:T(8,128)}) fusion(f32[16,128,256]{2,1,0:T(8,128)} %copy.106, f32[2048,256]{1,0:T(8,128)} %get-tuple-element.414, f32[256]{0:T(256)S(1)} %bitcast.142, pred[]{:T(512)S(6)} %compare.24, f32[16,128,256]{2,1,0:T(8,128)} %multiply_add_fusion.22, f32[2048,256]{1,0:T(8,128)} %get-tuple-element.413), kind=kLoop, calls=%fused_computation.3.clone.1 | loop fusion | flops 3145728 | bytes 12583937 | tf_op jit(solution)/shard_map/while/body/eval_jaxpr/add | solution.py:69
  275.2 4.0 fusion.89
  281.8 6.2 %fusion.90 = (f32[2048,256]{1,0:T(8,128)}, f32[2048,256]{1,0:T(8,128)}) fusion(f32[16,128,256]{2,1,0:T(8,128)} %copy.106, f32[2048,256]{1,0:T(8,128)} %get-tuple-element.414, f32[256]{0:T(256)S(1)} %bitcast.142, pred[]{:T(512)S(6)} %compare.24, f32[16,128,256]{2,1,0:T(8,128)} %multiply_add_fusion.22, f32[2048,256]{1,0:T(8,128)} %get-tuple-element.413), kind=kLoop, calls=%fused_computation.3.clone.1 | loop fusion | flops 3145728 | bytes 12583937 | tf_op jit(solution)/shard_map/while/body/eval_jaxpr/add | solution.py:69
  305.4 4.0 fusion.89
  312.0 6.2 %fusion.90 = (f32[2048,256]{1,0:T(8,128)}, f32[2048,256]{1,0:T(8,128)}) fusion(f32[16,128,256]{2,1,0:T(8,128)} %copy.106, f32[2048,256]{1,0:T(8,128)} %get-tuple-element.414, f32[256]{0:T(256)S(1)} %bitcast.142, pred[]{:T(512)S(6)} %compare.24, f32[16,128,256]{2,1,0:T(8,128)} %multiply_add_fusion.22, f32[2048,256]{1,0:T(8,128)} %get-tuple-element.413), kind=kLoop, calls=%fused_computation.3.clone.1 | loop fusion | flops 3145728 | bytes 12583937 | tf_op jit(solution)/shard_map/while/body/eval_jaxpr/add | solution.py:69
  335.7 4.0 fusion.89
  342.3 6.2 %fusion.90 = (f32[2048,256]{1,0:T(8,128)}, f32[2048,256]{1,0:T(8,128)}) fusion(f32[16,128,256]{2,1,0:T(8,128)} %copy.106, f32[2048,256]{1,0:T(8,128)} %get-tuple-element.414, f32[256]{0:T(256)S(1)} %bitcast.142, pred[]{:T(512)S(6)} %compare.24, f32[16,128,256]{2,1,0:T(8,128)} %multiply_add_fusion.22, f32[2048,256]{1,0:T(8,128)} %get-tuple-element.413), kind=kLoop, calls=%fused_computation.3.clone.1 | loop fusion | flops 3145728 | bytes 12583937 | tf_op jit(solution)/shard_map/while/body/eval_jaxpr/add | solution.py:69
  372.6 6.2 %fusion.90 = (f32[2048,256]{1,0:T(8,128)}, f32[2048,256]{1,0:T(8,128)}) fusion(f32[16,128,256]{2,1,0:T(8,128)} %copy.106, f32[2048,256]{1,0:T(8,128)} %get-tuple-element.414, f32[256]{0:T(256)S(1)} %bitcast.142, pred[]{:T(512)S(6)} %compare.24, f32[16,128,256]{2,1,0:T(8,128)} %multiply_add_fusion.22, f32[2048,256]{1,0:T(8,128)} %get-tuple-element.413), kind=kLoop, calls=%fused_computation.3.clone.1 | loop fusion | flops 3145728 | bytes 12583937 | tf_op jit(solution)/shard_map/while/body/eval_jaxpr/add | solution.py:69
  383.7 4.1 pad_maximum_fusion.7
  387.8 51.5 %all_to_all.30 = f32[2,2048,256]{2,0,1:T(2,128)S(1)} all-to-all(f32[2,2048,256]{2,0,1:T(2,128)S(1)} %pad_maximum_fusion.7), channel_id=1, replica_groups=mesh['ctx'=8,'tp'=4] {'ctx'}, dimensions={1} | all-to-all | bytes 8388608 | tf_op jit(solution)/shard_map/all_to_all | solution.py:117
  450.9 21.4 %fusion.46 = f32[1,128,2048]{2,0,1:T(1,128)S(1)} fusion(f32[256,1,2048]{2,0,1:T(8,128)S(1)} %bitcast.128, f32[1,383,2048]{2,1,0:T(8,128)S(1)} %copy-done.19), kind=kOutput, calls=%fused_computation.96 | convolution fusion | flops 805306368 | bytes 6283264 | tf_op jit(solution)/shard_map/conv_general_dilated | solution.py:19
  472.7 5.2 rev.16
  477.9 9.9 %all_gather.3 = f32[8,2048]{1,0:T(8,128)S(1)} all-gather(f32[8,256]{1,0:T(8,128)S(1)} %get-tuple-element.201), channel_id=1, replica_groups=mesh['ctx'=8,'tp'=4] {'ctx'}, dimensions={1}, use_global_device_ids=true | all-gather | bytes 73728 | tf_op jit(solution)/shard_map/all_gather | solution.py:122
  488.4 47.4 %all-reduce.20.cloned.1.call-done = f32[128,2048]{1,0:T(8,128)} async-done(((f32[128,2048]{1,0:T(8,128)}), f32[128,2048]{1,0:T(8,128)}) %all-reduce.20.cloned.1.call-update) | async-done | bytes 1048592 | tf_op jit(solution)/shard_map/psum | solution.py:133
  539.7 21.8 %fusion.38 = f32[1,256,2048]{2,0,1:T(1,128)S(1)} fusion(f32[1,383,2048]{2,1,0:T(8,128)S(1)} %maximum_bitcast_fusion, f32[128,1,2048]{2,0,1:T(8,128)S(1)} %bitcast.139), kind=kOutput, calls=%fused_computation.81 | convolution fusion | flops 805306368 | bytes 6283264 | tf_op jit(solution)/shard_map/conv_general_dilated | solution.py:19
  (750 shorter events, 188.3 us)
Async XLA Ops:
  7.2 61.6 %copy-start = (f32[8,2048]{1,0:T(8,128)S(1)}, f32[8,2048]{1,0:T(8,128)}, u32[]{:S(2)}) copy-start(f32[8,2048]{1,0:T(8,128)} %param.19) | copy-start | bytes 196612
  7.2 20.7 %copy-start.9 = (bf16[256,2048]{1,0:T(8,128)(2,1)S(1)}, bf16[256,2048]{1,0:T(8,128)(2,1)}, u32[]{:S(2)}) copy-start(bf16[256,2048]{1,0:T(8,128)(2,1)} %param.12) | copy-start | bytes 3145732
  7.2 20.7 %copy-start.11 = (bf16[256,2048]{1,0:T(8,128)(2,1)S(1)}, bf16[256,2048]{1,0:T(8,128)(2,1)}, u32[]{:S(2)}) copy-start(bf16[256,2048]{1,0:T(8,128)(2,1)} %param.13) | copy-start | bytes 3145732
  9.3 18.5 %collective-permute-start = (bf16[127,2048]{1,0:T(8,128)(2,1)}, bf16[127,2048]{1,0:T(8,128)(2,1)S(1)}, u32[]{:S(2)}, u32[]{:S(2)}) collective-permute-start(bf16[127,2048]{1,0:T(8,128)(2,1)} %slice.393), channel_id=1, source_target_pairs={{0,4},{4,8},{8,12},{12,16},{16,20},{20,24},{24,28},{1,5},{5,9},{9,... | collective-permute-start | bytes 1560584 | tf_op jit(solution)/shard_map/ppermute | solution.py:14
  13.7 14.1 %collective-permute-start.1 = (bf16[127,2048]{1,0:T(8,128)(2,1)}, bf16[127,2048]{1,0:T(8,128)(2,1)}, u32[]{:S(2)}, u32[]{:S(2)}) collective-permute-start(bf16[127,2048]{1,0:T(8,128)(2,1)} %slice.394), channel_id=1, source_target_pairs={{0,4},{4,8},{8,12},{12,16},{16,20},{20,24},{24,28},{1,5},{5,9},{9,... | collective-permute-start | bytes 1560584 | tf_op jit(solution)/shard_map/ppermute | solution.py:14
  31.3 21.6 %copy-start.13 = (bf16[256,2048]{1,0:T(8,128)(2,1)S(1)}, bf16[256,2048]{1,0:T(8,128)(2,1)}, u32[]{:S(2)}) copy-start(bf16[256,2048]{1,0:T(8,128)(2,1)} %param.15) | copy-start | bytes 3145732
  31.3 21.6 %copy-start.14 = (bf16[256,2048]{1,0:T(8,128)(2,1)S(1)}, bf16[256,2048]{1,0:T(8,128)(2,1)}, u32[]{:S(2)}) copy-start(bf16[256,2048]{1,0:T(8,128)(2,1)} %param.11) | copy-start | bytes 3145732
  31.3 21.6 %copy-start.16 = (bf16[256,2048]{1,0:T(8,128)(2,1)S(1)}, bf16[256,2048]{1,0:T(8,128)(2,1)}, u32[]{:S(2)}) copy-start(bf16[256,2048]{1,0:T(8,128)(2,1)} %param.16) | copy-start | bytes 3145732
  31.3 21.6 %copy-start.20 = (bf16[256,2048]{1,0:T(8,128)(2,1)S(1)}, bf16[256,2048]{1,0:T(8,128)(2,1)}, u32[]{:S(2)}) copy-start(bf16[256,2048]{1,0:T(8,128)(2,1)} %param.14) | copy-start | bytes 3145732
  64.1 53.7 %all-to-all-start = ((f32[2,256,2048]{1,0,2:T(2,128)}), f32[2,256,2048]{1,0,2:T(2,128)}, u32[]{:S(2)}, u32[]{:S(2)}) async-start(f32[2,256,2048]{1,0,2:T(2,128)} %copy.48), calls=%async_computation | async-start | bytes 8388608 | tf_op jit(solution)/shard_map/all_to_all | solution.py:107
  68.7 467.2 %all-reduce.20.cloned.1.call-start = ((), (), s32[]{:S(2)}) async-start(), calls=%async_computation.2 | async-start | bytes 2097152 | tf_op jit(solution)/shard_map/psum | solution.py:133
  131.9 6.1 %copy-start.23 = (f32[8]{0:T(128)S(1)}, f32[8]{0:T(128)}, u32[]{:S(2)}) copy-start(f32[8]{0:T(128)} %param.18) | copy-start | bytes 100
  162.0 5.0 copy-start.3
  167.0 4.1 copy-start.2
  191.0 6.2 %copy-start.3 = (f32[2048,256]{1,0:T(8,128)S(1)}, f32[2048,256]{1,0:T(8,128)}, u32[]{:S(2)}) copy-start(f32[2048,256]{1,0:T(8,128)} %copy-done.2) | copy-start | bytes 6291460 | tf_op jit(solution)/shard_map/while
  197.2 4.1 copy-start.2
  221.3 6.2 %copy-start.3 = (f32[2048,256]{1,0:T(8,128)S(1)}, f32[2048,256]{1,0:T(8,128)}, u32[]{:S(2)}) copy-start(f32[2048,256]{1,0:T(8,128)} %copy-done.2) | copy-start | bytes 6291460 | tf_op jit(solution)/shard_map/while
  227.5 4.1 copy-start.2
  251.5 6.2 %copy-start.3 = (f32[2048,256]{1,0:T(8,128)S(1)}, f32[2048,256]{1,0:T(8,128)}, u32[]{:S(2)}) copy-start(f32[2048,256]{1,0:T(8,128)} %copy-done.2) | copy-start | bytes 6291460 | tf_op jit(solution)/shard_map/while
  257.8 4.1 copy-start.2
  281.8 6.2 %copy-start.3 = (f32[2048,256]{1,0:T(8,128)S(1)}, f32[2048,256]{1,0:T(8,128)}, u32[]{:S(2)}) copy-start(f32[2048,256]{1,0:T(8,128)} %copy-done.2) | copy-start | bytes 6291460 | tf_op jit(solution)/shard_map/while
  288.0 4.1 copy-start.2
  312.0 6.2 %copy-start.3 = (f32[2048,256]{1,0:T(8,128)S(1)}, f32[2048,256]{1,0:T(8,128)}, u32[]{:S(2)}) copy-start(f32[2048,256]{1,0:T(8,128)} %copy-done.2) | copy-start | bytes 6291460 | tf_op jit(solution)/shard_map/while
  318.3 4.1 copy-start.2
  342.3 6.2 %copy-start.3 = (f32[2048,256]{1,0:T(8,128)S(1)}, f32[2048,256]{1,0:T(8,128)}, u32[]{:S(2)}) copy-start(f32[2048,256]{1,0:T(8,128)} %copy-done.2) | copy-start | bytes 6291460 | tf_op jit(solution)/shard_map/while
  348.5 4.1 copy-start.2
  372.6 6.2 %copy-start.3 = (f32[2048,256]{1,0:T(8,128)S(1)}, f32[2048,256]{1,0:T(8,128)}, u32[]{:S(2)}) copy-start(f32[2048,256]{1,0:T(8,128)} %copy-done.2) | copy-start | bytes 6291460 | tf_op jit(solution)/shard_map/while
  445.1 5.8 %copy-start.19 = (f32[1,383,2048]{2,1,0:T(8,128)S(1)}, f32[1,383,2048]{2,1,0:T(8,128)}, u32[]{:S(2)}) copy-start(f32[1,383,2048]{2,1,0:T(8,128)} %copy-done.18) | copy-start | bytes 9412612
  449.6 88.5 %collective-permute-start.2 = (f32[127,2048]{1,0:T(8,128)}, f32[127,2048]{1,0:T(8,128)}, u32[]{:S(2)}, u32[]{:S(2)}) collective-permute-start(f32[127,2048]{1,0:T(8,128)} %slice.517), channel_id=1, source_target_pairs={{4,0},{8,4},{12,8},{16,12},{20,16},{24,20},{28,24},{5,1},{9,5},{13... | collective-permute-start | bytes 3121160 | tf_op jit(solution)/shard_map/ppermute | solution.py:14
  539.7 21.8 %copy-start.10 = (bf16[256,2048]{1,0:T(8,128)(2,1)S(1)}, bf16[256,2048]{1,0:T(8,128)(2,1)}, u32[]{:S(2)}) copy-start(bf16[256,2048]{1,0:T(8,128)(2,1)} %param.12) | copy-start | bytes 3145732
  539.7 21.8 %copy-start.12 = (bf16[256,2048]{1,0:T(8,128)(2,1)S(1)}, bf16[256,2048]{1,0:T(8,128)(2,1)}, u32[]{:S(2)}) copy-start(bf16[256,2048]{1,0:T(8,128)(2,1)} %param.13) | copy-start | bytes 3145732
  539.7 24.3 %copy-start.1 = (f32[8,2048]{1,0:T(8,128)S(1)}, f32[8,2048]{1,0:T(8,128)}, u32[]{:S(2)}) copy-start(f32[8,2048]{1,0:T(8,128)} %param.19) | copy-start | bytes 196612
  (25 other events, 42.9 us)
Sparse Core Ops, SparseCore 0:
  478.0 57.7 all-reduce.19
where the time goes:
time: 574 us; the launch traced here: 571 us
  local copies, waits for them, and re-layouts  134 us (23%)
  other arithmetic  128 us (22%)
  matrix products  108 us (19%)
  waiting for transfers between devices  96.4 us (17%)
  blocking collectives  61.4 us (11%)
  between operations  14.4 us (3%)
  loops' own time  13.9 us (2%)
  starting transfers between devices  13.6 us (2%)
    conv_general_dilated x3, matrix products, depthwise(): lax.conv_general_dilated(signal[None], kernel[:, None, :], (1,), 'VALID',...  64.7 us
    all_to_all x1, blocking collectives, per_device(): lax.all_to_all(jnp.stack([conv_seq, back_seq]), 'ctx', split_axis=1, conc...  51.5 us
    all_to_all x1, waiting for transfers between devices, per_device(): lax.all_to_all(jnp.stack([li_input, li_cotan]), 'ctx', split_axis=2, conc...  49 us
    add x8, other arithmetic, one_mode(): back_sum = back_sum + residue_row[None, :] * reverse_states  48.2 us
    psum x1, waiting for transfers between devices, per_device(): tap_sum = lax.psum(tap_part, 'ctx')  47.4 us
    reduce_sum x8, other arithmetic, one_mode(): jnp.sum(inputs * reverse_states, 0)  32.1 us
    dot_general x8, matrix products, one_mode(): backward = jnp.einsum('jt,bjc->btc', toeplitz, co_blocks, precision=highest)  27.8 us
    add x8, other arithmetic, one_mode(): forward + lead_pows[None, :, None] * forward_in[:, None, :]  26.2 us
  transfers between devices with their start and end apart: 5, of which 2 were waited for; matrix products, arithmetic and copies ran while one was open for 7% of the time, Pallas kernels for 0%

commit v1 on v0

--- a/solution.py
+++ b/solution.py
@@ -6,6 +6,17 @@
 
 BLOCK = 128
 highest = lax.Precision.HIGHEST
+
+
+def cut_along(shard, dim, size):
+    before, after = (shard.shape[:dim], shard.shape[dim + 1 :])
+    return jnp.moveaxis(shard.reshape(*before, size, -1, *after), dim, 0)
+
+
+def joined_along(parts, dim):
+    parts = jnp.moveaxis(parts, 0, dim)
+    shape = parts.shape
+    return parts.reshape(*shape[:dim], shape[dim] * shape[dim + 1], *shape[dim + 2 :])
 
 
 def from_behind(value, axis, by):
@@ -104,9 +115,15 @@
     cotan = cotangent.astype(jnp.float32)
     li_input = key_second * mr_out
     li_cotan = cotan * query_li.astype(jnp.float32)
-    regrouped = lax.all_to_all(
-        jnp.stack([li_input, li_cotan]), "ctx", split_axis=2, concat_axis=1, tiled=True
-    )
+    array = jnp.stack([li_input, li_cotan])
+    length_2, index = (lax.axis_size("ctx"), lax.axis_index("ctx"))
+    pieces = cut_along(array, 2, length_2)
+    outs = [pieces[index]]
+    for step in range(1, length_2):
+        sent = pieces[index ^ step]
+        outs.append(lax.ppermute(sent, "ctx", [(i_2, i_2 ^ step) for i_2 in range(length_2)]))
+    pieces = jnp.stack(outs)[index ^ jnp.arange(length_2)]
+    regrouped = joined_along(pieces, 1)
     piece_cols = channels // devices_ctx
     local_residues = lax.dynamic_slice_in_dim(
         residues, lax.axis_index("ctx") * piece_cols, piece_cols, 1

time: 574 us -> 560 us (0.976)
  waiting for transfers between devices: 96.4 us -> 84 us
    all_to_all x1 -> x0, waiting for transfers between devices: 49 us -> none  [per_device(): lax.all_to_all(jnp.stack([li_input, li_cotan]), 'ctx', split_axis=2, conc...]
    ppermute x0 -> x7, waiting for transfers between devices: none -> 36.6 us  [per_device(): lax.ppermute(sent, 'ctx', [(i_2, i_2 ^ step) for i_2 in range(length_2)])]
    unnamed x43 -> x60, local copies, waits for them, and re-layouts: 5.08 us -> 18.7 us
    slice x2 -> x1, local copies, waits for them, and re-layouts: 15.6 us -> 4.01 us  [per_device(): regrouped[1]]
    ppermute x0 -> x7, starting transfers between devices: none -> 9.39 us  [per_device(): lax.ppermute(sent, 'ctx', [(i_2, i_2 ^ step) for i_2 in range(length_2)])]
  transfers between devices with their start and end apart: 5 -> 11, of which waited for: 2 -> 4; matrix products, arithmetic and copies ran while one was open for 7% -> 9% of each run, Pallas kernels for 0% -> 0%
where the time goes in v1:
time: 560 us; the launch traced here: 558 us
  local copies, waits for them, and re-layouts  131 us (23%)
  other arithmetic  126 us (22%)
  matrix products  108 us (19%)
  waiting for transfers between devices  84 us (15%)
  blocking collectives  61.6 us (11%)
  starting transfers between devices  18.4 us (3%)
  between operations  14.5 us (3%)
  loops' own time  14 us (2%)
    conv_general_dilated x3, matrix products, depthwise(): lax.conv_general_dilated(signal[None], kernel[:, None, :], (1,), 'VALID',...  64.7 us
    all_to_all x1, blocking collectives, per_device(): lax.all_to_all(jnp.stack([conv_seq, back_seq]), 'ctx', split_axis=1, conc...  51.7 us
    add x8, other arithmetic, one_mode(): back_sum = back_sum + residue_row[None, :] * reverse_states  48.2 us
    psum x1, waiting for transfers between devices, per_device(): tap_sum = lax.psum(tap_part, 'ctx')  47.4 us
    ppermute x7, waiting for transfers between devices, per_device(): lax.ppermute(sent, 'ctx', [(i_2, i_2 ^ step) for i_2 in range(length_2)])  36.6 us
    reduce_sum x8, other arithmetic, one_mode(): jnp.sum(inputs * reverse_states, 0)  32 us
    dot_general x8, matrix products, one_mode(): backward = jnp.einsum('jt,bjc->btc', toeplitz, co_blocks, precision=highest)  27.8 us
    add x8, other arithmetic, one_mode(): forward + lead_pows[None, :, None] * forward_in[:, None, :]  26.1 us
  transfers between devices with their start and end apart: 11, of which 4 were waited for; matrix products, arithmetic and copies ran while one was open for 9% of the time, Pallas kernels for 0%

profile of v1, /device:TPU:0, one launch (start us, length us, event | category | flops | bytes accessed | tf_op | source)
XLA Modules:
  0.0 557.7 jit_solution(15480097392421304041)
XLA Ops:
  14.5 4.5 collective-permute-start.1
  19.1 5.2 rev.15
  28.1 21.5 %fusion.47 = f32[1,256,2048]{2,0,1:T(1,128)S(1)} fusion(f32[1,383,2048]{2,1,0:T(8,128)S(1)} %convert_multiply_fusion, f32[128,1,2048]{2,0,1:T(8,128)S(1)} %bitcast.188), kind=kOutput, calls=%fused_computation.100 | convolution fusion | flops 805306368 | bytes 6283264 | tf_op jit(solution)/shard_map/conv_general_dilated | solution.py:30
  52.2 3.7 constant_dynamic-slice_fusion.1
  78.3 7.1 %collective-permute-done.4 = f32[2,256,256]{2,1,0:T(8,128)S(1)} collective-permute-done((f32[2,256,256]{2,1,0:T(8,128)S(1)}, f32[2,256,256]{2,1,0:T(8,128)S(1)}, u32[]{:S(2)}, u32[]{:S(2)}) %collective-permute-start.4) | collective-permute-done | bytes 524320 | tf_op jit(solution)/shard_map/ppermute | solution.py:124
  87.1 26.1 %collective-permute-done.6 = f32[2,256,256]{2,1,0:T(8,128)S(1)} collective-permute-done((f32[2,256,256]{2,1,0:T(8,128)S(1)}, f32[2,256,256]{2,1,0:T(8,128)S(1)}, u32[]{:S(2)}, u32[]{:S(2)}) %collective-permute-start.6) | collective-permute-done | bytes 524320 | tf_op jit(solution)/shard_map/ppermute | solution.py:124
  115.7 5.0 gather_fusion
  120.7 4.0 fusion.57
  124.7 240.8 %while.19 = (s32[]{:T(128)}, f32[2048,256]{1,0:T(8,128)}, f32[2048,256]{1,0:T(8,128)}, f32[8,256]{1,0:T(8,128)S(1)}, f32[8,256]{1,0:T(8,128)S(1)}, /*index=5*/f3...) while((s32[]{:T(128)}, f32[2048,256]{1,0:T(8,128)}, ...), condition=%wide.region_2.3_spmd.clone.clone, body=%wide.region_0.2_spmd.clone.clone.sunk | while | flops 1617155328 | bytes 74435056 | solution.py:90
  142.1 4.0 fusion.88
  148.8 4.9 fusion.89
  171.2 4.0 fusion.88
  177.8 6.2 %fusion.89 = (f32[2048,256]{1,0:T(8,128)}, f32[2048,256]{1,0:T(8,128)}) fusion(f32[16,128,256]{2,1,0:T(8,128)} %copy.121, f32[2048,256]{1,0:T(8,128)} %get-tuple-element.420, f32[256]{0:T(256)S(1)} %bitcast.194, pred[]{:T(512)S(6)} %compare.24, f32[16,128,256]{2,1,0:T(8,128)} %multiply_add_fusion.22, f32[2048,256]{1,0:T(8,128)} %get-tuple-element.419), kind=kLoop, calls=%fused_computation.4.clone.1 | loop fusion | flops 3145728 | bytes 12583937 | tf_op jit(solution)/shard_map/while/body/eval_jaxpr/add | solution.py:80
  201.4 4.0 fusion.88
  208.0 6.2 %fusion.89 = (f32[2048,256]{1,0:T(8,128)}, f32[2048,256]{1,0:T(8,128)}) fusion(f32[16,128,256]{2,1,0:T(8,128)} %copy.121, f32[2048,256]{1,0:T(8,128)} %get-tuple-element.420, f32[256]{0:T(256)S(1)} %bitcast.194, pred[]{:T(512)S(6)} %compare.24, f32[16,128,256]{2,1,0:T(8,128)} %multiply_add_fusion.22, f32[2048,256]{1,0:T(8,128)} %get-tuple-element.419), kind=kLoop, calls=%fused_computation.4.clone.1 | loop fusion | flops 3145728 | bytes 12583937 | tf_op jit(solution)/shard_map/while/body/eval_jaxpr/add | solution.py:80
  231.7 4.0 fusion.88
  238.3 6.2 %fusion.89 = (f32[2048,256]{1,0:T(8,128)}, f32[2048,256]{1,0:T(8,128)}) fusion(f32[16,128,256]{2,1,0:T(8,128)} %copy.121, f32[2048,256]{1,0:T(8,128)} %get-tuple-element.420, f32[256]{0:T(256)S(1)} %bitcast.194, pred[]{:T(512)S(6)} %compare.24, f32[16,128,256]{2,1,0:T(8,128)} %multiply_add_fusion.22, f32[2048,256]{1,0:T(8,128)} %get-tuple-element.419), kind=kLoop, calls=%fused_computation.4.clone.1 | loop fusion | flops 3145728 | bytes 12583937 | tf_op jit(solution)/shard_map/while/body/eval_jaxpr/add | solution.py:80
  261.9 4.0 fusion.88
  268.6 6.2 %fusion.89 = (f32[2048,256]{1,0:T(8,128)}, f32[2048,256]{1,0:T(8,128)}) fusion(f32[16,128,256]{2,1,0:T(8,128)} %copy.121, f32[2048,256]{1,0:T(8,128)} %get-tuple-element.420, f32[256]{0:T(256)S(1)} %bitcast.194, pred[]{:T(512)S(6)} %compare.24, f32[16,128,256]{2,1,0:T(8,128)} %multiply_add_fusion.22, f32[2048,256]{1,0:T(8,128)} %get-tuple-element.419), kind=kLoop, calls=%fused_computation.4.clone.1 | loop fusion | flops 3145728 | bytes 12583937 | tf_op jit(solution)/shard_map/while/body/eval_jaxpr/add | solution.py:80
  292.2 4.0 fusion.88
  298.8 6.2 %fusion.89 = (f32[2048,256]{1,0:T(8,128)}, f32[2048,256]{1,0:T(8,128)}) fusion(f32[16,128,256]{2,1,0:T(8,128)} %copy.121, f32[2048,256]{1,0:T(8,128)} %get-tuple-element.420, f32[256]{0:T(256)S(1)} %bitcast.194, pred[]{:T(512)S(6)} %compare.24, f32[16,128,256]{2,1,0:T(8,128)} %multiply_add_fusion.22, f32[2048,256]{1,0:T(8,128)} %get-tuple-element.419), kind=kLoop, calls=%fused_computation.4.clone.1 | loop fusion | flops 3145728 | bytes 12583937 | tf_op jit(solution)/shard_map/while/body/eval_jaxpr/add | solution.py:80
  322.4 4.0 fusion.88
  329.1 6.2 %fusion.89 = (f32[2048,256]{1,0:T(8,128)}, f32[2048,256]{1,0:T(8,128)}) fusion(f32[16,128,256]{2,1,0:T(8,128)} %copy.121, f32[2048,256]{1,0:T(8,128)} %get-tuple-element.420, f32[256]{0:T(256)S(1)} %bitcast.194, pred[]{:T(512)S(6)} %compare.24, f32[16,128,256]{2,1,0:T(8,128)} %multiply_add_fusion.22, f32[2048,256]{1,0:T(8,128)} %get-tuple-element.419), kind=kLoop, calls=%fused_computation.4.clone.1 | loop fusion | flops 3145728 | bytes 12583937 | tf_op jit(solution)/shard_map/while/body/eval_jaxpr/add | solution.py:80
  352.7 4.0 fusion.88
  359.3 6.2 %fusion.89 = (f32[2048,256]{1,0:T(8,128)}, f32[2048,256]{1,0:T(8,128)}) fusion(f32[16,128,256]{2,1,0:T(8,128)} %copy.121, f32[2048,256]{1,0:T(8,128)} %get-tuple-element.420, f32[256]{0:T(256)S(1)} %bitcast.194, pred[]{:T(512)S(6)} %compare.24, f32[16,128,256]{2,1,0:T(8,128)} %multiply_add_fusion.22, f32[2048,256]{1,0:T(8,128)} %get-tuple-element.419), kind=kLoop, calls=%fused_computation.4.clone.1 | loop fusion | flops 3145728 | bytes 12583937 | tf_op jit(solution)/shard_map/while/body/eval_jaxpr/add | solution.py:80
  370.5 4.1 pad_maximum_fusion.6
  374.6 51.7 %all_to_all.15 = f32[2,2048,256]{2,0,1:T(2,128)S(1)} all-to-all(f32[2,2048,256]{2,0,1:T(2,128)S(1)} %pad_maximum_fusion.6), channel_id=1, replica_groups=mesh['ctx'=8,'tp'=4] {'ctx'}, dimensions={1} | all-to-all | bytes 8388608 | tf_op jit(solution)/shard_map/all_to_all | solution.py:134
  437.8 21.4 %fusion.44 = f32[1,128,2048]{2,0,1:T(1,128)S(1)} fusion(f32[256,1,2048]{2,0,1:T(8,128)S(1)} %bitcast.172, f32[1,383,2048]{2,1,0:T(8,128)S(1)} %copy-done.18), kind=kOutput, calls=%fused_computation.96 | convolution fusion | flops 805306368 | bytes 6283264 | tf_op jit(solution)/shard_map/conv_general_dilated | solution.py:30
  459.5 5.2 rev.16
  464.7 9.9 %all_gather.3 = f32[8,2048]{1,0:T(8,128)S(1)} all-gather(f32[8,256]{1,0:T(8,128)S(1)} %get-tuple-element.201), channel_id=1, replica_groups=mesh['ctx'=8,'tp'=4] {'ctx'}, dimensions={1}, use_global_device_ids=true | all-gather | bytes 73728 | tf_op jit(solution)/shard_map/all_gather | solution.py:139
  475.2 47.4 %all-reduce.20.cloned.1.call-done = f32[128,2048]{1,0:T(8,128)} async-done(((f32[128,2048]{1,0:T(8,128)}), f32[128,2048]{1,0:T(8,128)}) %all-reduce.20.cloned.1.call-update) | async-done | bytes 1048592 | tf_op jit(solution)/shard_map/psum | solution.py:150
  526.6 21.8 %fusion.38 = f32[1,256,2048]{2,0,1:T(1,128)S(1)} fusion(f32[1,383,2048]{2,1,0:T(8,128)S(1)} %maximum_bitcast_fusion, f32[128,1,2048]{2,0,1:T(8,128)S(1)} %bitcast.187), kind=kOutput, calls=%fused_computation.81 | convolution fusion | flops 805306368 | bytes 6283264 | tf_op jit(solution)/shard_map/conv_general_dilated | solution.py:30
  (782 shorter events, 210.4 us)
Async XLA Ops:
  7.2 50.2 %copy-start = (f32[8,2048]{1,0:T(8,128)S(1)}, f32[8,2048]{1,0:T(8,128)}, u32[]{:S(2)}) copy-start(f32[8,2048]{1,0:T(8,128)} %param.19) | copy-start | bytes 196612
  7.2 11.9 %copy-start.19 = (f32[128,2048]{1,0:T(8,128)S(1)}, f32[128,2048]{1,0:T(8,128)}, u32[]{:S(2)}) copy-start(f32[128,2048]{1,0:T(8,128)} %param.17) | copy-start | bytes 3145732
  7.2 17.1 %copy-start.22 = (bf16[256,2048]{1,0:T(8,128)(2,1)S(1)}, bf16[256,2048]{1,0:T(8,128)(2,1)}, u32[]{:S(2)}) copy-start(bf16[256,2048]{1,0:T(8,128)(2,1)} %param.14) | copy-start | bytes 3145732
  7.2 17.0 %copy-start.15 = (bf16[256,2048]{1,0:T(8,128)(2,1)S(1)}, bf16[256,2048]{1,0:T(8,128)(2,1)}, u32[]{:S(2)}) copy-start(bf16[256,2048]{1,0:T(8,128)(2,1)} %param.16) | copy-start | bytes 3145732
  7.2 515.4 %all-reduce.20.cloned.1.call-start = ((), (), s32[]{:S(2)}) async-start(), calls=%async_computation.1 | async-start | bytes 2097152 | tf_op jit(solution)/shard_map/psum | solution.py:150
  9.4 16.2 %collective-permute-start = (bf16[127,2048]{1,0:T(8,128)(2,1)}, bf16[127,2048]{1,0:T(8,128)(2,1)}, u32[]{:S(2)}, u32[]{:S(2)}) collective-permute-start(bf16[127,2048]{1,0:T(8,128)(2,1)} %slice.393), channel_id=1, source_target_pairs={{0,4},{4,8},{8,12},{12,16},{16,20},{20,24},{24,28},{1,5},{5,9},{9,... | collective-permute-start | bytes 1560584 | tf_op jit(solution)/shard_map/ppermute | solution.py:25
  14.5 11.0 %collective-permute-start.1 = (bf16[127,2048]{1,0:T(8,128)(2,1)}, bf16[127,2048]{1,0:T(8,128)(2,1)}, u32[]{:S(2)}, u32[]{:S(2)}) collective-permute-start(bf16[127,2048]{1,0:T(8,128)(2,1)} %slice.394), channel_id=1, source_target_pairs={{0,4},{4,8},{8,12},{12,16},{16,20},{20,24},{24,28},{1,5},{5,9},{9,... | collective-permute-start | bytes 1560584 | tf_op jit(solution)/shard_map/ppermute | solution.py:25
  28.1 21.6 %copy-start.17 = (f32[1,383,2048]{2,1,0:T(8,128)}, f32[1,383,2048]{2,1,0:T(8,128)S(1)}, u32[]{:S(2)}) copy-start(f32[1,383,2048]{2,1,0:T(8,128)S(1)} %convert_multiply_fusion) | copy-start | bytes 9412612
  28.1 21.6 %copy-start.12 = (bf16[256,2048]{1,0:T(8,128)(2,1)S(1)}, bf16[256,2048]{1,0:T(8,128)(2,1)}, u32[]{:S(2)}) copy-start(bf16[256,2048]{1,0:T(8,128)(2,1)} %param.15) | copy-start | bytes 3145732
  28.1 21.6 %copy-start.13 = (bf16[256,2048]{1,0:T(8,128)(2,1)S(1)}, bf16[256,2048]{1,0:T(8,128)(2,1)}, u32[]{:S(2)}) copy-start(bf16[256,2048]{1,0:T(8,128)(2,1)} %param.11) | copy-start | bytes 3145732
  56.8 10.9 %collective-permute-start.2 = (f32[2,256,256]{2,1,0:T(8,128)}, f32[2,256,256]{2,1,0:T(8,128)}, u32[]{:S(2)}, u32[]{:S(2)}) collective-permute-start(f32[2,256,256]{2,1,0:T(8,128)} %bitcast.126), channel_id=1, source_target_pairs={{0,4},{4,0},{8,12},{12,8},{16,20},{20,16},{24,28},{28,24},{1,5},{5... | collective-permute-start | bytes 1572872 | tf_op jit(solution)/shard_map/ppermute | solution.py:124
  59.2 15.5 %collective-permute-start.3 = (f32[2,256,256]{2,1,0:T(8,128)}, f32[2,256,256]{2,1,0:T(8,128)}, u32[]{:S(2)}, u32[]{:S(2)}) collective-permute-start(f32[2,256,256]{2,1,0:T(8,128)} %bitcast.125), channel_id=1, source_target_pairs={{0,8},{4,12},{8,0},{12,4},{16,24},{20,28},{24,16},{28,20},{1,9},{5... | collective-permute-start | bytes 1572872 | tf_op jit(solution)/shard_map/ppermute | solution.py:124
  62.7 22.7 %collective-permute-start.4 = (f32[2,256,256]{2,1,0:T(8,128)S(1)}, f32[2,256,256]{2,1,0:T(8,128)S(1)}, u32[]{:S(2)}, u32[]{:S(2)}) collective-permute-start(f32[2,256,256]{2,1,0:T(8,128)S(1)} %bitcast.191), channel_id=1, source_target_pairs={{0,12},{4,8},{8,4},{12,0},{16,28},{20,24},{24,20},{28,16},{1,13},{... | collective-permute-start | bytes 1572872 | tf_op jit(solution)/shard_map/ppermute | solution.py:124
  64.8 21.5 %collective-permute-start.5 = (f32[2,256,256]{2,1,0:T(8,128)S(1)}, f32[2,256,256]{2,1,0:T(8,128)S(1)}, u32[]{:S(2)}, u32[]{:S(2)}) collective-permute-start(f32[2,256,256]{2,1,0:T(8,128)S(1)} %bitcast.193), channel_id=1, source_target_pairs={{0,16},{4,20},{8,24},{12,28},{16,0},{20,4},{24,8},{28,12},{1,17},{... | collective-permute-start | bytes 1572872 | tf_op jit(solution)/shard_map/ppermute | solution.py:124
  67.5 45.7 %collective-permute-start.6 = (f32[2,256,256]{2,1,0:T(8,128)S(1)}, f32[2,256,256]{2,1,0:T(8,128)S(1)}, u32[]{:S(2)}, u32[]{:S(2)}) collective-permute-start(f32[2,256,256]{2,1,0:T(8,128)S(1)} %bitcast.192), channel_id=1, source_target_pairs={{0,20},{4,16},{8,28},{12,24},{16,4},{20,0},{24,12},{28,8},{1,21},{... | collective-permute-start | bytes 1572872 | tf_op jit(solution)/shard_map/ppermute | solution.py:124
  67.7 46.3 %collective-permute-start.7 = (f32[2,256,256]{2,1,0:T(8,128)S(1)}, f32[2,256,256]{2,1,0:T(8,128)S(1)}, u32[]{:S(2)}, u32[]{:S(2)}) collective-permute-start(f32[2,256,256]{2,1,0:T(8,128)S(1)} %bitcast.190), channel_id=1, source_target_pairs={{0,24},{4,28},{8,16},{12,20},{16,8},{20,12},{24,0},{28,4},{1,25},{... | collective-permute-start | bytes 1572872 | tf_op jit(solution)/shard_map/ppermute | solution.py:124
  74.7 40.2 %collective-permute-start.8 = (f32[2,256,256]{2,1,0:T(8,128)S(1)}, f32[2,256,256]{2,1,0:T(8,128)S(1)}, u32[]{:S(2)}, u32[]{:S(2)}) collective-permute-start(f32[2,256,256]{2,1,0:T(8,128)S(1)} %bitcast.189), channel_id=1, source_target_pairs={{0,28},{4,24},{8,20},{12,16},{16,12},{20,8},{24,4},{28,0},{1,29},{... | collective-permute-start | bytes 1572872 | tf_op jit(solution)/shard_map/ppermute | solution.py:124
  148.8 5.0 copy-start.3
  153.7 4.1 copy-start.2
  177.8 6.2 %copy-start.3 = (f32[2048,256]{1,0:T(8,128)S(1)}, f32[2048,256]{1,0:T(8,128)}, u32[]{:S(2)}) copy-start(f32[2048,256]{1,0:T(8,128)} %copy-done.2) | copy-start | bytes 6291460 | tf_op jit(solution)/shard_map/while
  184.0 4.1 copy-start.2
  208.0 6.2 %copy-start.3 = (f32[2048,256]{1,0:T(8,128)S(1)}, f32[2048,256]{1,0:T(8,128)}, u32[]{:S(2)}) copy-start(f32[2048,256]{1,0:T(8,128)} %copy-done.2) | copy-start | bytes 6291460 | tf_op jit(solution)/shard_map/while
  238.3 6.2 %copy-start.3 = (f32[2048,256]{1,0:T(8,128)S(1)}, f32[2048,256]{1,0:T(8,128)}, u32[]{:S(2)}) copy-start(f32[2048,256]{1,0:T(8,128)} %copy-done.2) | copy-start | bytes 6291460 | tf_op jit(solution)/shard_map/while
  268.6 6.2 %copy-start.3 = (f32[2048,256]{1,0:T(8,128)S(1)}, f32[2048,256]{1,0:T(8,128)}, u32[]{:S(2)}) copy-start(f32[2048,256]{1,0:T(8,128)} %copy-done.2) | copy-start | bytes 6291460 | tf_op jit(solution)/shard_map/while
  298.8 6.2 %copy-start.3 = (f32[2048,256]{1,0:T(8,128)S(1)}, f32[2048,256]{1,0:T(8,128)}, u32[]{:S(2)}) copy-start(f32[2048,256]{1,0:T(8,128)} %copy-done.2) | copy-start | bytes 6291460 | tf_op jit(solution)/shard_map/while
  329.1 6.2 %copy-start.3 = (f32[2048,256]{1,0:T(8,128)S(1)}, f32[2048,256]{1,0:T(8,128)}, u32[]{:S(2)}) copy-start(f32[2048,256]{1,0:T(8,128)} %copy-done.2) | copy-start | bytes 6291460 | tf_op jit(solution)/shard_map/while
  359.3 6.2 %copy-start.3 = (f32[2048,256]{1,0:T(8,128)S(1)}, f32[2048,256]{1,0:T(8,128)}, u32[]{:S(2)}) copy-start(f32[2048,256]{1,0:T(8,128)} %copy-done.2) | copy-start | bytes 6291460 | tf_op jit(solution)/shard_map/while
  432.0 5.7 %copy-start.18 = (f32[1,383,2048]{2,1,0:T(8,128)S(1)}, f32[1,383,2048]{2,1,0:T(8,128)}, u32[]{:S(2)}) copy-start(f32[1,383,2048]{2,1,0:T(8,128)} %copy-done.17) | copy-start | bytes 9412612
  436.5 88.5 %collective-permute-start.9 = (f32[127,2048]{1,0:T(8,128)}, f32[127,2048]{1,0:T(8,128)}, u32[]{:S(2)}, u32[]{:S(2)}) collective-permute-start(f32[127,2048]{1,0:T(8,128)} %slice.519), channel_id=1, source_target_pairs={{4,0},{8,4},{12,8},{16,12},{20,16},{24,20},{28,24},{5,1},{9,5},{13... | collective-permute-start | bytes 3121160 | tf_op jit(solution)/shard_map/ppermute | solution.py:25
  526.5 21.8 %copy-start.10 = (bf16[256,2048]{1,0:T(8,128)(2,1)S(1)}, bf16[256,2048]{1,0:T(8,128)(2,1)}, u32[]{:S(2)}) copy-start(bf16[256,2048]{1,0:T(8,128)(2,1)} %param.12) | copy-start | bytes 3145732
  526.6 21.8 %copy-start.11 = (bf16[256,2048]{1,0:T(8,128)(2,1)S(1)}, bf16[256,2048]{1,0:T(8,128)(2,1)}, u32[]{:S(2)}) copy-start(bf16[256,2048]{1,0:T(8,128)(2,1)} %param.13) | copy-start | bytes 3145732
  526.6 24.3 %copy-start.1 = (f32[8,2048]{1,0:T(8,128)S(1)}, f32[8,2048]{1,0:T(8,128)}, u32[]{:S(2)}) copy-start(f32[8,2048]{1,0:T(8,128)} %param.19) | copy-start | bytes 196612
  (31 other events, 65.8 us)
Sparse Core Ops, SparseCore 0:
  464.8 57.7 all-reduce.19
